TPU v7x, 128 devices: a whole 4x4x4 slice. The times are simulated.
128 devices in a mesh: smp: 32 (over x, z, y_lo), col: 2 (over core), slab: 2 (over y_hi).
Axes of the slice: x: 4, y: 4 (y_hi: 2, y_lo: 2; y = y_hi * 2 + y_lo), z: 4, core: 2. Of those that a mesh axis runs over, the one named last changes fastest.
Arguments:
- jacobian: bfloat16 [1024, 32, 16384], P('smp', 'slab', 'col'), may hold values from -0.005722046 to 0.005722046
- local_energy: float32 [1024], P('smp'), may hold values from -6 to 6
Outputs:
- update: float32 [32, 16384], P('slab', ('col', 'smp'))
All inputs are finite; a program needn't handle non-finite values.
Results may differ from a plain program's by a relative error of at most 0.0085.
Values may be sent and summed in bfloat16 or wider, within the bound.
A program may use at most 192 MiB of HBM per device.

v0:
```python
import jax
import jax.numpy as jnp
from jax import lax
from jax.sharding import PartitionSpec as P

SLABS = 32
SLAB_COLS = 16384


def shards(jacobian, local_energy):
    energies = lax.all_gather(local_energy, "smp", axis=0, tiled=True)
    jacobian, energies = lax.optimization_barrier((jacobian, energies))
    samples = energies.shape[0]
    root_count = jnp.sqrt(jnp.float32(samples))
    eps = (energies - jnp.mean(energies)) / root_count
    columns = lax.all_to_all(jacobian, "smp", split_axis=2, concat_axis=0, tiled=True)
    slab_count = columns.shape[1]
    width = columns.shape[2]
    values = columns.astype(jnp.float32)
    mean_row = jnp.mean(values, axis=0, keepdims=True)
    centered = (
        ((values - mean_row) / root_count).astype(jnp.bfloat16).reshape(samples, slab_count * width)
    )
    partial_gram = jnp.dot(centered, centered.T, preferred_element_type=jnp.float32)
    gram = lax.psum(partial_gram, ("smp", "col", "slab"))
    shift = 0.01 * jnp.trace(gram) / samples
    factor = jnp.linalg.cholesky(gram + shift * jnp.eye(samples, dtype=jnp.float32))
    middle = lax.linalg.triangular_solve(factor, eps[:, None], left_side=True, lower=True)
    coeffs = lax.linalg.triangular_solve(
        factor, middle, left_side=True, lower=True, transpose_a=True
    )[:, 0]
    delta = jnp.dot(coeffs, centered.astype(jnp.float32), precision=lax.Precision.HIGHEST)
    squared = jnp.dot(
        coeffs,
        jnp.dot(gram, coeffs, precision=lax.Precision.HIGHEST),
        precision=lax.Precision.HIGHEST,
    )
    limit = 0.3 * jnp.sqrt(jnp.float32(SLABS * SLAB_COLS))
    scaled = -jnp.minimum(1.0, limit / jnp.sqrt(squared)) * delta
    return scaled.reshape(slab_count, width)


def solution(mesh):
    in_specs = (P("smp", "slab", "col"), P("smp"))
    out_specs = P("slab", ("col", "smp"))
    return jax.shard_map(shards, mesh=mesh, in_specs=in_specs, out_specs=out_specs, check_vma=False)
```

profile of v0, /device:TPU:1, one launch (start us, length us, event | category | flops | bytes accessed | tf_op | source)
XLA Modules:
  0.0 905.1 jit_solution(12480278940735346125)
XLA Ops:
  6.5 1.2 dynamic-slice.3
  9.3 70.8 %all-reduce.1 = f32[1024]{0:T(1024)S(1)} all-reduce(f32[1024]{0:T(1024)S(1)} %dynamic-update-slice.47), channel_id=1, replica_groups=mesh['smp'=32,'col'=2,'slab'=2] {'smp'}, use_global_device_ids=true, to_apply=%add.1 | all-reduce | flops 1024 | bytes 8192 | tf_op jit(solution)/shard_map/optimization_barrier | solution.py:12
  80.1 45.6 %copy.65 = bf16[32,16,8192]{0,1,2:T(8,128)(2,1)} copy(bf16[32,16,8192]{2,1,0:T(8,128)(2,1)} %param.2) | data formatting | bytes 16777216 | tf_op jit(solution)/shard_map/optimization_barrier | solution.py:12
  125.7 39.8 %reshape.346 = bf16[32,2,65536]{2,1,0:T(2,128)(2,1)} reshape(bf16[8192,16,32]{2,1,0:T(8,128)(2,1)} %bitcast.343) | data formatting | bytes 16777216
  165.5 86.4 %all_to_all.4 = bf16[32,2,65536]{2,1,0:T(2,128)(2,1)} all-to-all(bf16[32,2,65536]{2,1,0:T(2,128)(2,1)} %reshape.346), channel_id=1, replica_groups=mesh['smp'=32,'col'=2,'slab'=2] {'smp'}, dimensions={0} | all-to-all | bytes 16777216 | tf_op jit(solution)/shard_map/all_to_all | solution.py:16
  251.9 30.6 %reshape.347 = bf16[8192,16,32]{2,1,0:T(8,128)(2,1)} reshape(bf16[32,2,65536]{2,1,0:T(2,128)(2,1)} %all_to_all.4) | data formatting | bytes 16777216
  282.5 44.0 %copy.66 = f32[32,16,32,256]{3,1,0,2:T(8,128)} copy(bf16[32,16,32,256]{0,1,3,2:T(8,128)(2,1)} %bitcast.342) | data formatting | bytes 25165824 | tf_op jit(solution)/shard_map/convert_element_type | solution.py:19
  326.6 6.9 bitcast_reduce_fusion
  333.5 7.2 fusion.1
  340.6 3.2 copy-done.1
  343.8 16.8 %fusion.5 = f32[1024,1024]{0,1:T(8,128)} fusion(bf16[1024,16,256]{2,1,0:T(8,128)(2,1)S(1)} %bitcast.345), kind=kOutput, calls=%fused_computation.15 | convolution fusion | flops 8589934592 | bytes 12582912 | tf_op jit(solution)/shard_map/dot_general | solution.py:24
  362.1 12.2 %copy.98 = bf16[128,8,16,256]{3,1,2,0:T(8,128)(2,1)} copy(bf16[128,8,16,256]{3,2,1,0:T(8,128)(2,1)} %bitcast.346) | data formatting | bytes 16777216
  374.3 155.4 %all-reduce.4.cloned.1.call-done = f32[1024,1024]{0,1:T(8,128)} async-done(((f32[1024,1024]{0,1:T(8,128)}), f32[1024,1024]{0,1:T(8,128)}) %all-reduce.4.cloned.1.call-update) | async-done | bytes 4194320 | tf_op jit(solution)/shard_map/psum | solution.py:25
  529.7 2.9 select_reduce_fusion
  533.2 4.8 select_add_fusion
  538.0 5.7 copy.70
  543.8 4.5 fusion.4
  548.3 2.0 copy-done.2
  550.2 11.7 %cholesky.222 = f32[128,128]{1,0:T(8,128)S(1)} custom-call(f32[128,128]{1,0:T(8,128)S(1)} %cholesky.577), custom_call_target="Cholesky" | custom-call | tf_op jit(solution)/shard_map/jit(cholesky)/cholesky | solution.py:27
  562.0 9.8 %custom-call.64 = f32[1,128,128]{1,2,0:T(8,128)S(1)} custom-call(f32[1,128,128]{2,1,0:T(8,128)S(1)} %get-tuple-element.56), custom_call_target="InvertDiagBlocksLowerTriangular" | custom-call | tf_op jit(solution)/shard_map/jit(cholesky)/cholesky | solution.py:27
  571.8 1.5 fusion.45
  573.3 1.6 convolution_subtract_fusion
  574.9 11.7 %cholesky.243 = f32[128,128]{1,0:T(8,128)S(1)} custom-call(f32[128,128]{1,0:T(8,128)S(1)} %cholesky.581), custom_call_target="Cholesky" | custom-call | tf_op jit(solution)/shard_map/jit(cholesky)/cholesky | solution.py:27
  587.2 2.5 cholesky.254
  589.7 9.8 %custom-call.65 = f32[1,128,128]{1,2,0:T(8,128)S(1)} custom-call(f32[1,128,128]{2,1,0:T(8,128)S(1)} %get-tuple-element.54), custom_call_target="InvertDiagBlocksLowerTriangular" | custom-call | tf_op jit(solution)/shard_map/jit(cholesky)/cholesky | solution.py:27
  601.0 1.3 convolution_dynamic-update-slice_fusion
  602.3 2.7 convolution_subtract_fusion.1
  605.1 11.7 %cholesky.466 = f32[128,128]{1,0:T(8,128)S(1)} custom-call(f32[128,128]{1,0:T(8,128)S(1)} %cholesky.586), custom_call_target="Cholesky" | custom-call | tf_op jit(solution)/shard_map/jit(cholesky)/cholesky | solution.py:27
  617.6 9.8 %custom-call.66 = f32[1,128,128]{1,2,0:T(8,128)S(1)} custom-call(f32[1,128,128]{2,1,0:T(8,128)S(1)} %get-tuple-element.52), custom_call_target="InvertDiagBlocksLowerTriangular" | custom-call | tf_op jit(solution)/shard_map/jit(cholesky)/cholesky | solution.py:27
  628.6 3.3 convolution_subtract_fusion.2
  632.0 11.7 %cholesky.485 = f32[128,128]{1,0:T(8,128)S(1)} custom-call(f32[128,128]{1,0:T(8,128)S(1)} %cholesky.591), custom_call_target="Cholesky" | custom-call | tf_op jit(solution)/shard_map/jit(cholesky)/cholesky | solution.py:27
  644.5 9.8 %custom-call.67 = f32[1,128,128]{1,2,0:T(8,128)S(1)} custom-call(f32[1,128,128]{2,1,0:T(8,128)S(1)} %get-tuple-element.50), custom_call_target="InvertDiagBlocksLowerTriangular" | custom-call | tf_op jit(solution)/shard_map/jit(cholesky)/cholesky | solution.py:27
  655.4 3.2 convolution_subtract_fusion.3
  658.6 12.1 %cholesky.504 = f32[128,128]{1,0:T(8,128)S(1)} custom-call(f32[128,128]{1,0:T(8,128)S(1)} %cholesky.596), custom_call_target="Cholesky" | custom-call | tf_op jit(solution)/shard_map/jit(cholesky)/cholesky | solution.py:27
  671.4 9.8 %custom-call.68 = f32[1,128,128]{1,2,0:T(8,128)S(1)} custom-call(f32[1,128,128]{2,1,0:T(8,128)S(1)} %get-tuple-element.48), custom_call_target="InvertDiagBlocksLowerTriangular" | custom-call | tf_op jit(solution)/shard_map/jit(cholesky)/cholesky | solution.py:27
  682.4 3.1 convolution_subtract_fusion.4
  685.5 11.7 %cholesky.524 = f32[128,128]{1,0:T(8,128)S(1)} custom-call(f32[128,128]{1,0:T(8,128)S(1)} %cholesky.601), custom_call_target="Cholesky" | custom-call | tf_op jit(solution)/shard_map/jit(cholesky)/cholesky | solution.py:27
  698.0 9.8 %custom-call.69 = f32[1,128,128]{1,2,0:T(8,128)S(1)} custom-call(f32[1,128,128]{2,1,0:T(8,128)S(1)} %get-tuple-element.46), custom_call_target="InvertDiagBlocksLowerTriangular" | custom-call | tf_op jit(solution)/shard_map/jit(cholesky)/cholesky | solution.py:27
  708.8 2.8 convolution_subtract_fusion.5
  711.6 11.7 %cholesky.544 = f32[128,128]{1,0:T(8,128)S(1)} custom-call(f32[128,128]{1,0:T(8,128)S(1)} %cholesky.606), custom_call_target="Cholesky" | custom-call | tf_op jit(solution)/shard_map/jit(cholesky)/cholesky | solution.py:27
  724.1 9.8 %custom-call.70 = f32[1,128,128]{1,2,0:T(8,128)S(1)} custom-call(f32[1,128,128]{2,1,0:T(8,128)S(1)} %get-tuple-element.44), custom_call_target="InvertDiagBlocksLowerTriangular" | custom-call | tf_op jit(solution)/shard_map/jit(cholesky)/cholesky | solution.py:27
  734.8 2.1 convolution_subtract_fusion.6
  736.9 11.7 %cholesky.562 = f32[128,128]{1,0:T(8,128)S(1)} custom-call(f32[128,128]{1,0:T(8,128)S(1)} %convolution_subtract_fusion.6), custom_call_target="Cholesky" | custom-call | tf_op jit(solution)/shard_map/jit(cholesky)/cholesky | solution.py:27
  758.8 4.9 select_select_fusion
  763.7 24.5 %while.1 = (s32[]{:T(128)}, f32[1024,1024]{0,1:T(8,128)}, s32[8,2]{0,1:T(2,128)S(1)}, f32[8,128,128]{2,1,0:T(8,128)S(1)}, s32[]{:T(128)}) while((s32[]{:T(128)}, f32[1024,1024]{0,1:T(8,128)}, s32[8,2]{0,1:T(2,128)S(1)}, f32[8,128,128]{2,1,0:T(8,128)S(1)}, s32[]{:T(128)}) %tuple.54), condition=%wide.while_cond, body=%wide.while_body.sunk | while | flops 2 | bytes 393321 | solution.py:29
  764.3 2.3 dynamic-slice.8
  767.4 2.3 dynamic-slice.8
  770.5 2.3 dynamic-slice.8
  773.5 2.3 dynamic-slice.8
  776.6 2.3 dynamic-slice.8
  779.7 2.3 dynamic-slice.8
  782.8 2.3 dynamic-slice.8
  785.8 2.2 dynamic-slice.8
  788.2 78.8 %custom-call.71 = f32[8,128,128]{1,2,0:T(8,128)S(1)} custom-call(f32[8,128,128]{2,1,0:T(8,128)S(1)} %get-tuple-element.16), custom_call_target="InvertDiagBlocksLowerTriangular" | custom-call | tf_op jit(solution)/shard_map/triangular_solve | solution.py:29
  872.5 1.3 fusion.34
  874.0 1.3 fusion.24
  875.5 1.4 fusion.18
  879.9 1.2 fusion.32
  881.3 1.3 fusion.26
  882.9 1.4 fusion.30
  884.6 1.4 fusion.28
  886.3 1.5 fusion.20
  888.1 2.3 fusion.125
  891.7 5.7 fusion.126
  (137 shorter events, 35.8 us)
Async XLA Ops:
  6.5 523.2 %all-reduce.4.cloned.1.call-start = ((), (), s32[]{:S(2)}) async-start(), calls=%async_computation.1 | async-start | bytes 8388608 | tf_op jit(solution)/shard_map/psum | solution.py:25
  340.6 3.2 copy-start.1
  548.3 2.0 copy-start.2
  867.0 21.1 %copy-start = (f32[1024,1024]{0,1:T(8,128)S(1)}, f32[1024,1024]{0,1:T(8,128)}, u32[]{:S(2)}) copy-start(f32[1024,1024]{0,1:T(8,128)} %all-reduce.4.cloned.1.call-done) | copy-start | bytes 12582916
Sparse Core Ops, SparseCore 0:
  360.8 168.8 all-reduce.3
where the time goes:
time: 912 us; the launch traced here: 905 us
  other arithmetic  279 us (31%)
  local copies, waits for them, and re-layouts  219 us (24%)
  blocking collectives  157 us (17%)
  waiting for transfers between devices  155 us (17%)
  matrix products  72.4 us (8%)
  between operations  21.5 us (2%)
    another operation x30, other arithmetic, shards(): jnp.linalg.cholesky(gram + shift * jnp.eye(samples, dtype=jnp.float32))  168 us
    psum x1, waiting for transfers between devices, shards(): gram = lax.psum(partial_gram, ('smp', 'col', 'slab'))  155 us
    unnamed x30, local copies, waits for them, and re-layouts  90.2 us
    all_to_all x1, blocking collectives, shards(): lax.all_to_all(jacobian, 'smp', split_axis=2, concat_axis=0, tiled=True)  86.4 us
    another operation x3, other arithmetic, shards(): lax.linalg.triangular_solve(factor, middle, left_side=True, lower=True, t...  83.7 us
    optimization_barrier x1, blocking collectives, shards(): jacobian, energies = lax.optimization_barrier((jacobian, energies))  70.8 us
    optimization_barrier x1, local copies, waits for them, and re-layouts, shards(): jacobian, energies = lax.optimization_barrier((jacobian, energies))  45.6 us
    convert_element_type x1, local copies, waits for them, and re-layouts, shards(): values = columns.astype(jnp.float32)  44 us
  transfers between devices with their start and end apart: 1, of which 1 were waited for; matrix products, arithmetic and copies ran while one was open for 1% of the time, Pallas kernels for 0%

commit v1 on v0

--- a/solution.py
+++ b/solution.py
@@ -22,7 +22,7 @@
         ((values - mean_row) / root_count).astype(jnp.bfloat16).reshape(samples, slab_count * width)
     )
     partial_gram = jnp.dot(centered, centered.T, preferred_element_type=jnp.float32)
-    gram = lax.psum(partial_gram, ("smp", "col", "slab"))
+    gram = lax.psum(lax.psum(partial_gram, ("col", "slab")), "smp")
     shift = 0.01 * jnp.trace(gram) / samples
     factor = jnp.linalg.cholesky(gram + shift * jnp.eye(samples, dtype=jnp.float32))
     middle = lax.linalg.triangular_solve(factor, eps[:, None], left_side=True, lower=True)

time: 912 us -> 1240 us (1.36)
  the two profiles are of different devices: /device:TPU:1 before, /device:TPU:16 now
where the time goes in v1:
time: 1240 us
  waiting for transfers between devices  473 us (38%)
  other arithmetic  279 us (22%)
  local copies, waits for them, and re-layouts  219 us (18%)
  blocking collectives  171 us (14%)
  matrix products  72.2 us (6%)
  between operations  21.6 us (2%)
    psum x2, waiting for transfers between devices, shards(): gram = lax.psum(lax.psum(partial_gram, ('col', 'slab')), 'smp')  473 us
    another operation x30, other arithmetic, shards(): jnp.linalg.cholesky(gram + shift * jnp.eye(samples, dtype=jnp.float32))  168 us
    unnamed x30, local copies, waits for them, and re-layouts  90.2 us
    all_to_all x1, blocking collectives, shards(): lax.all_to_all(jacobian, 'smp', split_axis=2, concat_axis=0, tiled=True)  87.4 us
    optimization_barrier x1, blocking collectives, shards(): jacobian, energies = lax.optimization_barrier((jacobian, energies))  83.8 us
    another operation x3, other arithmetic, shards(): lax.linalg.triangular_solve(factor, middle, left_side=True, lower=True, t...  83.7 us
    optimization_barrier x1, local copies, waits for them, and re-layouts, shards(): jacobian, energies = lax.optimization_barrier((jacobian, energies))  45.6 us
    convert_element_type x1, local copies, waits for them, and re-layouts, shards(): values = columns.astype(jnp.float32)  44 us
  transfers between devices with their start and end apart: 2, of which 2 were waited for; matrix products, arithmetic and copies ran while one was open for 1% of the time, Pallas kernels for 0%

profile of v1, /device:TPU:16, one launch (start us, length us, event | category | flops | bytes accessed | tf_op | source)
XLA Modules:
  0.0 1236.5 jit_solution(13328443616182696846)
XLA Ops:
  6.5 1.2 dynamic-slice.3
  9.3 83.8 %all-reduce.1 = f32[1024]{0:T(1024)S(1)} all-reduce(f32[1024]{0:T(1024)S(1)} %dynamic-update-slice.47), channel_id=1, replica_groups=mesh['smp'=32,'col'=2,'slab'=2] {'smp'}, use_global_device_ids=true, to_apply=%add.1 | all-reduce | flops 1024 | bytes 8192 | tf_op jit(solution)/shard_map/optimization_barrier | solution.py:12
  93.1 45.6 %copy.65 = bf16[32,16,8192]{0,1,2:T(8,128)(2,1)} copy(bf16[32,16,8192]{2,1,0:T(8,128)(2,1)} %param.2) | data formatting | bytes 16777216 | tf_op jit(solution)/shard_map/optimization_barrier | solution.py:12
  138.6 39.8 %reshape.346 = bf16[32,2,65536]{2,1,0:T(2,128)(2,1)} reshape(bf16[8192,16,32]{2,1,0:T(8,128)(2,1)} %bitcast.343) | data formatting | bytes 16777216
  178.4 87.4 %all_to_all.4 = bf16[32,2,65536]{2,1,0:T(2,128)(2,1)} all-to-all(bf16[32,2,65536]{2,1,0:T(2,128)(2,1)} %reshape.346), channel_id=1, replica_groups=mesh['smp'=32,'col'=2,'slab'=2] {'smp'}, dimensions={0} | all-to-all | bytes 16777216 | tf_op jit(solution)/shard_map/all_to_all | solution.py:16
  265.8 30.6 %reshape.347 = bf16[8192,16,32]{2,1,0:T(8,128)(2,1)} reshape(bf16[32,2,65536]{2,1,0:T(2,128)(2,1)} %all_to_all.4) | data formatting | bytes 16777216
  296.4 44.0 %copy.66 = f32[32,16,32,256]{3,1,0,2:T(8,128)} copy(bf16[32,16,32,256]{0,1,3,2:T(8,128)(2,1)} %bitcast.342) | data formatting | bytes 25165824 | tf_op jit(solution)/shard_map/convert_element_type | solution.py:19
  340.5 6.9 bitcast_reduce_fusion
  347.4 7.2 fusion.1
  354.6 3.2 copy-done.1
  357.8 16.6 %fusion.5 = f32[1024,1024]{0,1:T(8,128)} fusion(bf16[1024,16,256]{2,1,0:T(8,128)(2,1)S(1)} %bitcast.345), kind=kOutput, calls=%fused_computation.15 | convolution fusion | flops 8589934592 | bytes 12582912 | tf_op jit(solution)/shard_map/dot_general | solution.py:24
  374.6 157.3 %all-reduce.5.cloned.1.call-done = f32[1024,1024]{0,1:T(8,128)} async-done(((f32[1024,1024]{0,1:T(8,128)}), f32[1024,1024]{0,1:T(8,128)}) %all-reduce.5.cloned.1.call-update) | async-done | bytes 4194320 | tf_op jit(solution)/shard_map/psum | solution.py:25
  533.3 12.2 copy.98
  545.6 315.6 %all-reduce.7.cloned.1.call-done = f32[1024,1024]{0,1:T(8,128)} async-done(((f32[1024,1024]{0,1:T(8,128)}), f32[1024,1024]{0,1:T(8,128)}) %all-reduce.7.cloned.1.call-update) | async-done | bytes 4194320 | tf_op jit(solution)/shard_map/psum | solution.py:25
  861.2 2.9 select_reduce_fusion
  864.6 4.8 select_add_fusion
  869.5 5.7 copy.70
  875.2 4.5 fusion.4
  879.7 2.0 copy-done.2
  881.7 11.7 cholesky.222
  893.4 9.8 custom-call.64
  903.3 1.5 fusion.45
  904.8 1.6 convolution_subtract_fusion
  906.4 11.7 cholesky.243
  918.7 2.5 cholesky.254
  921.2 9.8 custom-call.65
  932.5 1.3 convolution_dynamic-update-slice_fusion
  933.8 2.7 convolution_subtract_fusion.1
  936.5 11.7 cholesky.466
  949.0 9.8 custom-call.66
  960.0 3.3 convolution_subtract_fusion.2
  963.4 11.7 cholesky.485
  975.9 9.8 custom-call.67
  986.8 3.2 convolution_subtract_fusion.3
  990.0 12.1 cholesky.504
  1002.9 9.8 custom-call.68
  1013.8 3.1 convolution_subtract_fusion.4
  1016.9 11.7 cholesky.524
  1029.4 9.8 custom-call.69
  1040.2 2.8 convolution_subtract_fusion.5
  1043.0 11.7 cholesky.544
  1055.5 9.8 custom-call.70
  1066.3 2.1 convolution_subtract_fusion.6
  1068.4 11.7 cholesky.562
  1090.3 4.9 select_select_fusion
  1095.1 24.5 %while.1 = (s32[]{:T(128)}, f32[1024,1024]{0,1:T(8,128)}, s32[8,2]{0,1:T(2,128)S(1)}, f32[8,128,128]{2,1,0:T(8,128)S(1)}, s32[]{:T(128)}) while((s32[]{:T(128)}, f32[1024,1024]{0,1:T(8,128)}, s32[8,2]{0,1:T(2,128)S(1)}, f32[8,128,128]{2,1,0:T(8,128)S(1)}, s32[]{:T(128)}) %tuple.54), condition=%wide.while_cond, body=%wide.while_body.sunk | while | flops 2 | bytes 393321 | solution.py:29
  1095.8 2.3 dynamic-slice.8
  1098.9 2.3 dynamic-slice.8
  1101.9 2.3 dynamic-slice.8
  1105.0 2.3 dynamic-slice.8
  1108.1 2.3 dynamic-slice.8
  1111.1 2.3 dynamic-slice.8
  1114.2 2.3 dynamic-slice.8
  1117.3 2.2 dynamic-slice.8
  1119.6 78.8 %custom-call.71 = f32[8,128,128]{1,2,0:T(8,128)S(1)} custom-call(f32[8,128,128]{2,1,0:T(8,128)S(1)} %get-tuple-element.16), custom_call_target="InvertDiagBlocksLowerTriangular" | custom-call | tf_op jit(solution)/shard_map/triangular_solve | solution.py:29
  1203.9 1.3 fusion.34
  1205.4 1.3 fusion.24
  1206.9 1.4 fusion.18
  1212.8 1.3 fusion.26
  1214.3 1.4 fusion.30
  1216.0 1.4 fusion.28
  1217.7 1.5 fusion.20
  1219.6 2.3 fusion.125
  1223.2 5.7 fusion.126
  (140 shorter events, 37.3 us)
Async XLA Ops:
  6.5 525.4 %all-reduce.5.cloned.1.call-start = ((), (), s32[]{:S(2)}) async-start(), calls=%async_computation.1 | async-start | bytes 8388608 | tf_op jit(solution)/shard_map/psum | solution.py:25
  354.5 3.2 copy-start.1
  374.3 486.8 %all-reduce.7.cloned.1.call-start = ((), (), s32[]{:S(2)}) async-start(), calls=%async_computation.2 | async-start | bytes 8388608 | tf_op jit(solution)/shard_map/psum | solution.py:25
  879.7 2.0 copy-start.2
  1198.4 21.1 %copy-start = (f32[1024,1024]{0,1:T(8,128)S(1)}, f32[1024,1024]{0,1:T(8,128)}, u32[]{:S(2)}) copy-start(f32[1024,1024]{0,1:T(8,128)} %all-reduce.7.cloned.1.call-done) | copy-start | bytes 12582916
Sparse Core Ops, SparseCore 0:
  374.5 157.3 all-reduce.4
  534.5 326.5 all-reduce.6
